TPU v7x, 32 devices: a whole 2x2x4 slice. The times are simulated.
32 devices in a mesh: seq: 8 (over z, y), dp: 4 (over x, core).
Axes of the slice: x: 2, y: 2, z: 4, core: 2. Of those that a mesh axis runs over, the one named last changes fastest.
Arguments:
- out_grad: bfloat16 [4, 1536, 4096], P('dp', 'seq'), may hold values from -6 to 6
- w_out: bfloat16 [2048, 4096], P('dp'), may hold values from -0.125 to 0.125
- queries: bfloat16 [4, 1536, 2048], P('dp', 'seq'), may hold values from -6 to 6
- keys: bfloat16 [4, 1536, 2048], P('dp', 'seq'), may hold values from -6 to 6
- values: bfloat16 [4, 1536, 2048], P('dp', 'seq'), may hold values from -6 to 6
- keep_bits: int32 [4, 1536, 128], P('dp', 'seq'), may hold values from 0 to 65535
- query_later: float32 [4, 16, 128, 128], P('dp'), may hold values from -1.8 to 1.8
Outputs:
- query_grad: bfloat16 [4, 1536, 2048], P('dp', 'seq')
- key_grad: bfloat16 [4, 1536, 2048], P('dp', 'seq')
- value_grad: bfloat16 [4, 1536, 2048], P('dp', 'seq')
All inputs are finite; a program needn't handle non-finite values.
Results may differ from a plain program's by a relative error of at most 0.0058.
Values may be sent and summed in bfloat16 or wider, within the bound.
A program may use at most 192 MiB of HBM per device.

v0:
```python
import jax
import jax.numpy as jnp
from jax import lax
from jax.sharding import PartitionSpec as P

HD = 128


def carried_in(part, axis, combine, identity, reverse):
    count = lax.axis_size(axis)
    place = lax.axis_index(axis)
    ahead = count - 1 - place if reverse else place
    gathered = lax.all_gather(part, axis)
    state = jnp.zeros_like(part) + jnp.asarray(identity, part.dtype)

    def one(step, state):
        source = count - 1 - step if reverse else step
        return combine(state, lax.dynamic_index_in_dim(gathered, source, 0, False))

    return lax.fori_loop(0, ahead, one, state)


def unpack_flags(word_bits, count):
    bit_shift = jnp.arange(16, dtype=jnp.int32)
    flags = word_bits[..., None] >> bit_shift & 1
    return flags.reshape(word_bits.shape[:-1] + (count,)).astype(jnp.float32)


def add_states(earlier, later):
    return earlier + later


def body(out_grad, w_out, queries, keys, values, keep_bits, query_later):
    tok_count = out_grad.shape[1]
    inner_width = queries.shape[2]
    head_size = HD
    head_count = inner_width // head_size
    grad_tokens = out_grad[0]
    projected = lax.dot_general(
        grad_tokens,
        lax.all_gather(w_out, "dp", axis=0, tiled=True),
        (((1,), (1,)), ((), ())),
        preferred_element_type=jnp.float32,
    )
    keep_mask = unpack_flags(keep_bits[0], inner_width)
    position = (lax.axis_index("seq") * tok_count + jnp.arange(tok_count, dtype=jnp.int32)).astype(
        jnp.float32
    )
    row_scale = 2.0 / jnp.sqrt(head_size * (position + 1.0))
    gated = (projected * keep_mask * row_scale[:, None]).astype(jnp.bfloat16)
    gated_heads = gated.reshape(tok_count, head_count, head_size)
    query_heads = queries[0].reshape(tok_count, head_count, head_size)
    key_heads = keys[0].reshape(tok_count, head_count, head_size)
    value_heads = values[0].reshape(tok_count, head_count, head_size)
    key_state = jnp.einsum(
        "thi,thj->hij", key_heads, value_heads, preferred_element_type=jnp.float32
    )
    query_state = jnp.einsum(
        "thi,thj->hij", query_heads, gated_heads, preferred_element_type=jnp.float32
    )
    zero_state = jnp.zeros_like(key_state)
    key_before = carried_in(key_state, "seq", add_states, zero_state, False)
    query_after = carried_in(query_state, "seq", add_states, zero_state, True)
    query_after = query_after + query_later[0]
    key_before_b = key_before.astype(jnp.bfloat16)
    query_after_b = query_after.astype(jnp.bfloat16)
    causal_mask = (jnp.arange(tok_count)[:, None] >= jnp.arange(tok_count)[None, :]).astype(
        jnp.float32
    )
    grad_scores = (
        jnp.einsum("thj,shj->hts", gated_heads, value_heads, preferred_element_type=jnp.float32)
        * causal_mask
    ).astype(jnp.bfloat16)
    attn_scores = (
        jnp.einsum("thj,shj->hts", query_heads, key_heads, preferred_element_type=jnp.float32)
        * causal_mask
    ).astype(jnp.bfloat16)
    query_grad = jnp.einsum(
        "hts,shi->thi", grad_scores, key_heads, preferred_element_type=jnp.float32
    )
    query_grad = query_grad + jnp.einsum(
        "thj,hij->thi", gated_heads, key_before_b, preferred_element_type=jnp.float32
    )
    key_grad = jnp.einsum(
        "hts,thi->shi", grad_scores, query_heads, preferred_element_type=jnp.float32
    )
    key_grad = key_grad + jnp.einsum(
        "shj,hij->shi", value_heads, query_after_b, preferred_element_type=jnp.float32
    )
    value_grad = jnp.einsum(
        "hts,thj->shj", attn_scores, gated_heads, preferred_element_type=jnp.float32
    )
    value_grad = value_grad + jnp.einsum(
        "shi,hij->shj", key_heads, query_after_b, preferred_element_type=jnp.float32
    )

    def merge_heads(tensor):
        return tensor.reshape(1, tok_count, inner_width).astype(jnp.bfloat16)

    return (merge_heads(query_grad), merge_heads(key_grad), merge_heads(value_grad))


def solution(mesh):
    in_specs = (
        P("dp", "seq", None),
        P("dp", None),
        P("dp", "seq", None),
        P("dp", "seq", None),
        P("dp", "seq", None),
        P("dp", "seq", None),
        P("dp", None, None, None),
    )
    out_specs = (P("dp", "seq", None), P("dp", "seq", None), P("dp", "seq", None))
    return jax.shard_map(body, mesh=mesh, in_specs=in_specs, out_specs=out_specs, check_vma=False)
```

profile of v0, /device:TPU:0, one launch (start us, length us, event | category | flops | bytes accessed | tf_op | source)
XLA Modules:
  0.0 395.9 jit_solution(10310405240292140329)
XLA Ops:
  7.2 0.0 copy-start
  7.2 0.0 copy-start.10
  7.2 0.0 all-gather.6.cloned.1.call-start
  7.2 0.7 all-gather.6.cloned.1.call-update
  7.9 0.0 all-gather.8.cloned.1.call-start
  8.0 0.0 copy-start.11
  8.0 0.5 copy-done.10
  8.4 0.2 copy.71
  8.6 0.0 copy-start.2
  8.6 0.6 copy-done.11
  9.2 0.2 copy.70
  9.3 0.0 copy-start.13
  9.3 1.5 fusion.21
  10.9 0.0 copy-done.2
  10.9 0.0 all-gather.8.cloned.1.call-update
  10.9 0.0 all-gather.10.cloned.1.call-start
  11.0 0.0 copy-done.13
  11.0 0.1 copy.45
  11.1 1.6 shift_right_arithmetic.23
  12.6 2.9 copy.46
  15.6 0.1 shift_right_arithmetic.26
  15.6 0.0 copy-done.12
  15.6 1.2 copy.72
  16.8 101.4 %all-gather.6.cloned.1.call-done = bf16[2048,4096]{1,0:T(8,128)(2,1)} async-done(((bf16[512,4096]{1,0:T(8,128)(2,1)}), bf16[2048,4096]{1,0:T(8,128)(2,1)}) %all-gather.6.cloned.1.call-update) | async-done | bytes 16777232 | tf_op jit(solution)/shard_map/all_gather | solution.py:41
  118.2 0.0 copy-done
  118.2 11.9 %fusion.7 = bf16[24,16,8,128]{3,2,1,0:T(8,128)(2,1)S(1)} fusion(s32[192,2048]{1,0:T(8,128)} %copy.46, bf16[2048,4096]{1,0:T(8,128)(2,1)} %all-gather.6.cloned.1.call-done, bf16[1,192,4096]{2,1,0:T(8,128)(2,1)S(1)} %copy-done, f32[192]{0:T(256)S(1)} %rsqrt_multiply_fusion, s32[2048]{0:T(1024)S(1)} %shift_right_arithmetic.26), kind=kOutput, calls=%fused_computation.16 | convolution fusion | flops 3223584768 | bytes 20718336 | tf_op jit(solution)/shard_map/dot_general | solution.py:39
  130.2 0.0 copy-start.6
  130.2 1.9 convolution_bitcast_fusion
  132.1 1.3 copy.58
  133.5 0.0 all-gather.10.cloned.1.call-update
  133.5 0.7 fusion.35
  134.2 111.2 %all-gather.8.cloned.1.call-done = f32[128,128,128]{2,1,0:T(8,128)} async-done(((f32[16,128,128]{2,1,0:T(8,128)}), f32[128,128,128]{2,1,0:T(8,128)}) %all-gather.8.cloned.1.call-update) | async-done | bytes 8388624 | tf_op jit(solution)/shard_map/all_gather | solution.py:13
  245.3 0.1 broadcast_in_dim.2.clone
  245.4 0.0 copy-done.6
  245.5 0.0 copy-start.3
  245.5 1.8 multiply_convert_fusion.1
  247.3 0.0 copy-start.7
  247.3 0.6 fusion.33
  247.9 0.6 copy-done.7
  248.5 0.5 fusion.3
  249.0 0.5 copy.53
  249.5 1.2 convert_element_type.86
  250.7 3.2 fusion.18
  253.9 3.7 fusion.5
  257.6 113.0 %all-gather.10.cloned.1.call-done = f32[128,128,128]{2,1,0:T(8,128)} async-done(((f32[16,128,128]{2,1,0:T(8,128)}), f32[128,128,128]{2,1,0:T(8,128)}) %all-gather.10.cloned.1.call-update) | async-done | bytes 8388624 | tf_op jit(solution)/shard_map/all_gather | solution.py:13
  370.6 0.1 broadcast_in_dim.2.clone.1
  370.7 10.8 %while.23 = (s32[]{:T(128)}, f32[16,128,128]{2,1,0:T(8,128)S(1)}, s32[]{:T(128)}, f32[8,16,128,128]{3,2,1,0:T(8,128)}, s32[]{:T(128)}, /*index=5*/s32[]{:T(128)}, s32[]{:T(128)}, s32[]{:T(128)}) while((s32[]{:T(128)}, f32[16,128,128]{2,1,0:T(8,128)S(1)}, s32[]{:T(128)}, f32[8,16,128,128]{3,2,1,0:T(8,128)}, s32[]{:T(128)}, ...), condition=%wide.region_3.4_spmd, body=%wide.region_2.3_spmd.sunk | while | flops 262150 | bytes 3145863 | solution.py:20
  370.7 1.5 bitcast_add_fusion.8
  372.3 1.5 bitcast_add_fusion.8
  373.8 1.5 bitcast_add_fusion.8
  375.3 1.5 bitcast_add_fusion.8
  376.8 1.5 bitcast_add_fusion.8
  378.3 1.5 bitcast_add_fusion.8
  379.8 1.5 bitcast_add_fusion.8
  381.5 0.0 copy-start.5
  381.5 1.5 fusion.10
  383.0 0.0 copy-done.5
  383.1 0.4 copy-done.8
  383.5 0.4 fusion.6
  383.9 0.5 copy.66
  384.4 1.2 convert_element_type.93
  385.6 2.0 fusion.2
  387.6 0.5 copy.60
  388.1 1.2 convert_element_type.89
  (12 shorter events, 0.0 us)
Async XLA Ops:
  7.2 111.1 %copy-start = (bf16[1,192,4096]{2,1,0:T(8,128)(2,1)S(1)}, bf16[1,192,4096]{2,1,0:T(8,128)(2,1)}, u32[]{:S(2)}) copy-start(bf16[1,192,4096]{2,1,0:T(8,128)(2,1)} %param.11) | copy-start | bytes 4718596
  7.2 1.3 copy-start.10
  7.2 111.0 %all-gather.6.cloned.1.call-start = ((), (), s32[]{:S(2)}) async-start(), calls=%async_computation | async-start | bytes 20971520 | tf_op jit(solution)/shard_map/all_gather | solution.py:41
  7.9 237.4 %all-gather.8.cloned.1.call-start = ((), (), s32[]{:S(2)}) async-start(), calls=%async_computation.1 | async-start | bytes 9437184 | tf_op jit(solution)/shard_map/all_gather | solution.py:13
  8.0 1.2 copy-start.11
  8.6 2.3 copy-start.2
  9.3 1.6 copy-start.13
  10.9 359.7 %all-gather.10.cloned.1.call-start = ((), (), s32[]{:S(2)}) async-start(), calls=%async_computation.2 | async-start | bytes 9437184 | tf_op jit(solution)/shard_map/all_gather | solution.py:13
  12.6 3.0 copy-start.12
  130.2 115.3 %copy-start.6 = (bf16[24,16,8,128]{3,2,1,0:T(8,128)(2,1)}, bf16[24,16,8,128]{3,2,1,0:T(8,128)(2,1)S(1)}, u32[]{:S(2)}) copy-start(bf16[24,16,8,128]{3,2,1,0:T(8,128)(2,1)S(1)} %fusion.7) | copy-start | bytes 2359300
  245.5 1.9 copy-start.3
  247.3 1.1 copy-start.7
  250.7 3.2 copy-start.4
  250.7 3.2 copy-start.9
  381.5 1.5 copy-start.5
  381.5 2.0 copy-start.8
  385.6 3.7 copy-start.1
Sparse Core Ops, SparseCore 0:
  9.6 108.6 all-gather.5
  120.4 124.9 all-gather.7
  247.5 123.1 all-gather.9
where the time goes:
time: 397 us; the launch traced here: 396 us
  waiting for transfers between devices  326 us (82%)
  matrix products  27.6 us (7%)
  local copies, waits for them, and re-layouts  14.9 us (4%)
  between operations  14 us (4%)
  other arithmetic  12.6 us (3%)
    all_gather x2, waiting for transfers between devices, carried_in(): gathered = lax.all_gather(part, axis)  224 us
    all_gather x1, waiting for transfers between devices, body(): lax.all_gather(w_out, 'dp', axis=0, tiled=True)  101 us
    dot_general x1, matrix products, body(): lax.dot_general(grad_tokens, lax.all_gather(w_out, 'dp', axis=0, tiled=Tr...  11.9 us
    add x7, other arithmetic, add_states(): return earlier + later  10.4 us
  transfers between devices with their start and end apart: 3, of which 3 were waited for; matrix products, arithmetic and copies ran while one was open for 9% of the time, Pallas kernels for 0%

commit v1 on v0

--- a/solution.py
+++ b/solution.py
@@ -1,9 +1,28 @@
+import functools
 import jax
 import jax.numpy as jnp
 from jax import lax
 from jax.sharding import PartitionSpec as P
 
 HD = 128
+
+
+def region_wait(q_in, peer_axis):
+    kept_arr = lax.axis_size(peer_axis)
+    before = lax.axis_index(peer_axis)
+    f_next, s_next = (kept_arr, before)
+    val, view_out = (q_in, 1)
+    while view_out < f_next:
+        reached = tuple(((idx, idx ^ view_out) for idx in range(f_next)))
+        local_part = lax.ppermute(val, peer_axis, reached)
+        met_up = jnp.concatenate([val, local_part], 0)
+        last = jnp.concatenate([local_part, val], 0)
+        val = jnp.where(s_next & view_out == 0, met_up, last)
+        view_out = 2 * view_out
+    return val
+
+
+ratios_store = functools.partial(region_wait, peer_axis="dp")
 
 
 def carried_in(part, axis, combine, identity, reverse):
@@ -38,7 +57,7 @@
     grad_tokens = out_grad[0]
     projected = lax.dot_general(
         grad_tokens,
-        lax.all_gather(w_out, "dp", axis=0, tiled=True),
+        ratios_store(w_out),
         (((1,), (1,)), ((), ())),
         preferred_element_type=jnp.float32,
     )

time: 397 us -> 380 us (0.957)
  waiting for transfers between devices: 326 us -> 291 us
  other arithmetic: 12.6 us -> 23.6 us
    ppermute x0 -> x2, waiting for transfers between devices: none -> 177 us  [region_wait(): local_part = lax.ppermute(val, peer_axis, reached)]
    all_gather x2, waiting for transfers between devices: 224 us -> 113 us  [carried_in(): gathered = lax.all_gather(part, axis)]
    all_gather x1 -> x0, waiting for transfers between devices: 101 us -> none  [body(): lax.all_gather(w_out, 'dp', axis=0, tiled=True)]
    select_n x0 -> x1, other arithmetic: none -> 11.7 us  [region_wait(): val = jnp.where(s_next & view_out == 0, met_up, last)]
  transfers between devices with their start and end apart: 3 -> 4, of which waited for: 3 -> 3; matrix products, arithmetic and copies ran while one was open for 9% -> 14% of each run, Pallas kernels for 0% -> 0%
where the time goes in v1:
time: 380 us; the launch traced here: 379 us
  waiting for transfers between devices  291 us (77%)
  matrix products  29.6 us (8%)
  other arithmetic  23.6 us (6%)
  local copies, waits for them, and re-layouts  17.4 us (5%)
  between operations  14.2 us (4%)
    ppermute x2, waiting for transfers between devices, region_wait(): local_part = lax.ppermute(val, peer_axis, reached)  177 us
    all_gather x2, waiting for transfers between devices, carried_in(): gathered = lax.all_gather(part, axis)  113 us
    dot_general x1, matrix products, body(): lax.dot_general(grad_tokens, ratios_store(w_out), (((1,), (1,)), ((), ())...  13.7 us
    select_n x1, other arithmetic, region_wait(): val = jnp.where(s_next & view_out == 0, met_up, last)  11.7 us
    add x7, other arithmetic, add_states(): return earlier + later  10.4 us
  transfers between devices with their start and end apart: 4, of which 3 were waited for; matrix products, arithmetic and copies ran while one was open for 14% of the time, Pallas kernels for 0%

profile of v1, /device:TPU:0, one launch (start us, length us, event | category | flops | bytes accessed | tf_op | source)
XLA Modules:
  0.0 379.2 jit_solution(15412036983045742754)
XLA Ops:
  7.2 0.0 copy-start
  7.2 0.0 all-gather.5.cloned.1.call-start
  7.2 0.5 collective-permute-start
  7.7 1.3 copy.70
  9.0 1.3 copy.71
  10.3 1.5 fusion.30
  11.9 0.0 all-gather.5.cloned.1.call-update
  11.9 0.0 all-gather.7.cloned.1.call-start
  12.0 0.0 copy-start.7
  12.0 2.9 collective-permute-done
  14.9 11.7 %maximum_select_fusion.2 = bf16[1024,4096]{1,0:T(8,128)(2,1)} fusion(bf16[512,4096]{1,0:T(8,128)(2,1)} %collective-permute-done, bf16[512,4096]{1,0:T(8,128)(2,1)} %param.12, pred[]{:T(512)S(6)} %eq.7), kind=kLoop, calls=%fused_computation.10 | loop fusion | flops 37748736 | bytes 16777216 | tf_op jit(solution)/shard_map/jit(_where)/select_n | solution.py:20
  26.6 2.9 collective-permute-start.1
  29.4 0.0 copy-done.7
  29.4 0.1 copy.45
  29.5 1.5 shift_right_arithmetic.23
  31.1 2.8 copy.46
  33.8 0.1 shift_right_arithmetic.26
  33.9 2.2 copy.72
  36.1 0.0 copy-start.3
  36.1 174.3 %collective-permute-done.1 = bf16[1024,4096]{1,0:T(8,128)(2,1)} collective-permute-done((bf16[1024,4096]{1,0:T(8,128)(2,1)}, bf16[1024,4096]{1,0:T(8,128)(2,1)}, u32[]{:S(2)}, u32[]{:S(2)}) %collective-permute-start.1) | collective-permute-done | bytes 8388640 | tf_op jit(solution)/shard_map/ppermute | solution.py:17
  210.5 0.0 copy-done
  210.5 13.7 %fusion.16 = bf16[24,16,8,128]{3,2,1,0:T(8,128)(2,1)S(1)} fusion(s32[192,2048]{1,0:T(8,128)} %copy.46, bf16[1,192,4096]{2,1,0:T(8,128)(2,1)S(1)} %copy-done, bf16[1024,4096]{1,0:T(8,128)(2,1)} %collective-permute-done.1, bf16[1024,4096]{1,0:T(8,128)(2,1)} %maximum_select_fusion.2, pred[]{:T(512)S(6)} %eq.6, f32[192]{0:T(256)S(1)} %rsqrt_multiply_fusion, ...), kind=kOutput, calls=%fused_computation.26 | convolution fusion | flops 3299082240 | bytes 20718336 | tf_op jit(solution)/shard_map/dot_general | solution.py:58
  224.1 0.0 copy-start.2
  224.2 0.9 copy-done.2
  225.0 0.0 copy-done.3
  225.0 0.5 convolution_bitcast_fusion
  225.5 1.3 copy.58
  226.9 0.0 all-gather.7.cloned.1.call-update
  226.9 0.0 copy-start.4
  226.9 1.8 multiply_convert_fusion.1
  228.7 1.7 fusion.42
  230.5 0.0 copy-done.4
  230.5 1.9 fusion.27
  232.4 3.6 fusion.14
  236.0 0.0 all-gather.5.cloned.1.call-done
  236.0 0.1 broadcast_in_dim.2.clone
  236.1 2.4 fusion.12
  238.5 0.5 copy.53
  239.0 1.2 convert_element_type.86
  240.3 113.3 %all-gather.7.cloned.1.call-done = f32[128,128,128]{2,1,0:T(8,128)} async-done(((f32[16,128,128]{2,1,0:T(8,128)}), f32[128,128,128]{2,1,0:T(8,128)}) %all-gather.7.cloned.1.call-update) | async-done | bytes 8388624 | tf_op jit(solution)/shard_map/all_gather | solution.py:32
  353.6 0.1 broadcast_in_dim.2.clone.1
  353.7 10.8 %while.23 = (s32[]{:T(128)}, f32[16,128,128]{2,1,0:T(8,128)S(1)}, s32[]{:T(128)}, f32[8,16,128,128]{3,2,1,0:T(8,128)}, s32[]{:T(128)}, /*index=5*/s32[]{:T(128)}, s32[]{:T(128)}, s32[]{:T(128)}) while((s32[]{:T(128)}, f32[16,128,128]{2,1,0:T(8,128)S(1)}, s32[]{:T(128)}, f32[8,16,128,128]{3,2,1,0:T(8,128)}, s32[]{:T(128)}, ...), condition=%wide.region_3.4_spmd, body=%wide.region_2.3_spmd.sunk | while | flops 262150 | bytes 3145871 | solution.py:39
  353.7 1.5 bitcast_add_fusion.8
  355.2 1.5 bitcast_add_fusion.8
  356.7 1.5 bitcast_add_fusion.8
  358.2 1.5 bitcast_add_fusion.8
  359.7 1.5 bitcast_add_fusion.8
  361.3 1.5 bitcast_add_fusion.8
  362.8 1.5 bitcast_add_fusion.8
  364.4 0.0 copy-start.5
  364.5 1.5 fusion.19
  365.9 0.2 copy-done.5
  366.2 0.0 copy-start.6
  366.2 0.5 fusion.11
  366.7 0.3 copy-done.6
  367.0 0.5 copy.60
  367.5 0.0 copy-start.1
  367.5 1.2 convert_element_type.89
  368.7 1.9 fusion.15
  370.7 0.5 copy.66
  371.2 1.2 convert_element_type.93
  372.4 0.0 copy-done.1
  (4 shorter events, 0.0 us)
Async XLA Ops:
  7.2 203.3 %copy-start = (bf16[1,192,4096]{2,1,0:T(8,128)(2,1)S(1)}, bf16[1,192,4096]{2,1,0:T(8,128)(2,1)}, u32[]{:S(2)}) copy-start(bf16[1,192,4096]{2,1,0:T(8,128)(2,1)} %param.11) | copy-start | bytes 4718596
  7.2 228.8 %all-gather.5.cloned.1.call-start = ((), (), s32[]{:S(2)}) async-start(), calls=%async_computation | async-start | bytes 9437184 | tf_op jit(solution)/shard_map/all_gather | solution.py:32
  7.2 7.6 %collective-permute-start = (bf16[512,4096]{1,0:T(8,128)(2,1)}, bf16[512,4096]{1,0:T(8,128)(2,1)}, u32[]{:S(2)}, u32[]{:S(2)}) collective-permute-start(bf16[512,4096]{1,0:T(8,128)(2,1)} %param.12), channel_id=1, source_target_pairs={{0,1},{1,0},{2,3},{3,2},{4,5},{5,4},{6,7},{7,6},{8,9},{9,8},{10,11... | collective-permute-start | bytes 12582920 | tf_op jit(solution)/shard_map/ppermute | solution.py:17
  11.9 341.7 %all-gather.7.cloned.1.call-start = ((), (), s32[]{:S(2)}) async-start(), calls=%async_computation.1 | async-start | bytes 9437184 | tf_op jit(solution)/shard_map/all_gather | solution.py:32
  12.0 17.5 %copy-start.7 = (s32[1,192,128]{2,1,0:T(8,128)S(1)}, s32[1,192,128]{2,1,0:T(8,128)}, u32[]{:S(2)}) copy-start(s32[1,192,128]{2,1,0:T(8,128)} %param.16) | copy-start | bytes 294916
  26.6 183.9 %collective-permute-start.1 = (bf16[1024,4096]{1,0:T(8,128)(2,1)}, bf16[1024,4096]{1,0:T(8,128)(2,1)}, u32[]{:S(2)}, u32[]{:S(2)}) collective-permute-start(bf16[1024,4096]{1,0:T(8,128)(2,1)} %maximum_select_fusion.2), channel_id=1, source_target_pairs={{0,2},{1,3},{2,0},{3,1},{4,6},{5,7},{6,4},{7,5},{8,10},{9,11},{10,... | collective-permute-start | bytes 25165832 | tf_op jit(solution)/shard_map/ppermute | solution.py:17
  36.1 188.9 %copy-start.3 = (bf16[24,8,16,128]{3,2,1,0:T(8,128)(2,1)S(1)}, bf16[24,8,16,128]{3,2,1,0:T(8,128)(2,1)}, u32[]{:S(2)}) copy-start(bf16[24,8,16,128]{3,2,1,0:T(8,128)(2,1)} %copy.72) | copy-start | bytes 2359300
  224.1 0.9 copy-start.2
  226.9 3.6 copy-start.4
  364.4 1.7 copy-start.5
  366.2 0.8 copy-start.6
  367.5 4.9 %copy-start.1 = (bf16[1,192,4096]{2,1,0:T(8,128)(2,1)S(1)}, bf16[1,192,4096]{2,1,0:T(8,128)(2,1)}, u32[]{:S(2)}) copy-start(bf16[1,192,4096]{2,1,0:T(8,128)(2,1)} %param.11) | copy-start | bytes 4718596
Sparse Core Ops, SparseCore 0:
  12.0 127.3 all-gather.4
  227.0 126.5 all-gather.6
